TPU v7x, 32 devices: a whole 2x2x4 slice. The times are simulated.
32 devices in a mesh: pair: 8 (over z, y), aux: 4 (over x, core).
Axes of the slice: x: 2, y: 2, z: 4, core: 2. Of those that a mesh axis runs over, the one named last changes fastest.
Arguments:
- x_panels: float32 [1024, 1024], P(None, 'pair'), may hold values from -0.25 to 0.25
- xbar_panels: float32 [1024, 1024], P(None, 'pair'), may hold values from -6 to 6
- bbar_below: float32 [4096, 1024], P('aux', 'pair'), may hold values from -6 to 6
- l_below: float32 [4096, 1024], P(('aux', 'pair')), may hold values from -0.09375 to 0.09375
- l_cross: float32 [512, 512], P('pair'), may hold values from -0.25 to 0.25
- dinv: float32 [2, 512, 512], P(None, 'pair'), as said below
Outputs:
- bbar_panels: float32 [1024, 1024], P(None, 'pair')
- lbar_below: float32 [4096, 1024], P(('aux', 'pair'))
- lbar_diag: float32 [2, 512, 512], P(None, 'pair')
- lbar_cross: float32 [512, 512], P('pair')
Inputs may be any that keep to these rules, and one draw needn't show every extreme that they name: Each dinv[k] is lower triangular with a positive diagonal.
All inputs are finite; a program needn't handle non-finite values.
Results may differ from a plain program's by a relative error of at most 0.00013.
Values sent between devices are 32-bit elements; how exact they have to be, the bound alone decides.
No kernel may reach another device: no remote copies, remote signals or barrier semaphores. Data moves between devices by JAX's collectives and lax.ppermute only.
A program may use at most 64 MiB of HBM per device.

v0:
```python
import jax
import jax.numpy as jnp
from jax import lax
from jax.sharding import PartitionSpec as P


def fold_with(right_side, pieces):
    return lax.dot_general(
        pieces,
        right_side,
        (((0,), (0,)), ((), ())),
        precision=lax.Precision.HIGHEST,
        preferred_element_type=jnp.float32,
    )


def body(x_panels, xbar_panels, bbar_below, l_below, l_cross, dinv):
    panel = dinv.shape[2]
    precise = lax.Precision.HIGHEST
    contract_cols = (((1,), (1,)), ((), ()))

    def below_correction(first, count):
        columns = l_below[:, first : first + count]
        folded = fold_with(bbar_below, lax.all_gather(columns, "pair", axis=0, tiled=True))
        return lax.psum(folded, "aux")

    def solve_panel(index, right_side):
        return fold_with(right_side, lax.all_gather(dinv[index], "pair", axis=0, tiled=True))

    lbar_below = lax.psum_scatter(
        -lax.dot_general(
            bbar_below,
            x_panels,
            contract_cols,
            precision=precise,
            preferred_element_type=jnp.float32,
        ),
        "pair",
        scatter_dimension=0,
        tiled=True,
    )
    late_corr = below_correction(panel, panel)
    bbar_late = solve_panel(1, xbar_panels[panel:] - late_corr)
    cross_term = fold_with(bbar_late, lax.all_gather(l_cross, "pair", axis=0, tiled=True))
    early_corr = below_correction(0, panel)
    bbar_early = solve_panel(0, xbar_panels[:panel] - early_corr - cross_term)
    x_early = x_panels[:panel]
    x_late = x_panels[panel:]
    diag_early = -lax.dot_general(
        bbar_early, x_early, contract_cols, precision=precise, preferred_element_type=jnp.float32
    )
    diag_late = -lax.dot_general(
        bbar_late, x_late, contract_cols, precision=precise, preferred_element_type=jnp.float32
    )
    cross_block = -lax.dot_general(
        bbar_late, x_early, contract_cols, precision=precise, preferred_element_type=jnp.float32
    )
    stacked = jnp.stack([diag_early, diag_late, cross_block])
    summed = lax.psum_scatter(stacked, "pair", scatter_dimension=1, tiled=True)
    bbar_panels = jnp.concatenate([bbar_early, bbar_late], axis=0)
    return (bbar_panels, lbar_below, summed[:2], summed[2])


def solution(mesh):
    in_specs = (
        P(None, "pair"),
        P(None, "pair"),
        P("aux", "pair"),
        P(("aux", "pair"), None),
        P("pair", None),
        P(None, "pair", None),
    )
    out_specs = (P(None, "pair"), P(("aux", "pair"), None), P(None, "pair", None), P("pair", None))
    return jax.shard_map(body, mesh=mesh, in_specs=in_specs, out_specs=out_specs, check_vma=False)
```

profile of v0, /device:TPU:0, one launch (start us, length us, event | category | flops | bytes accessed | tf_op | source)
XLA Modules:
  0.0 450.9 jit_solution(8527038155251425231)
XLA Ops:
  7.2 1.9 fusion.13
  10.0 1.7 fusion.14
  11.7 50.8 %all-gather.8.cloned.1.call-done = f32[1024,512]{1,0:T(8,128)} async-done(((f32[128,512]{1,0:T(8,128)}), f32[1024,512]{1,0:T(8,128)}) %all-gather.8.cloned.1.call-update) | async-done | bytes 2097168 | tf_op jit(solution)/shard_map/all_gather | solution.py:24
  62.5 5.7 %fusion.15 = f32[512,128]{1,0:T(8,128)} fusion(f32[1024,512]{1,0:T(8,128)} %all-gather.8.cloned.1.call-done, f32[1024,128]{1,0:T(8,128)S(1)} %copy-done), kind=kOutput, calls=%fused_computation.23 | convolution fusion | flops 805306368 | bytes 2883584 | tf_op jit(solution)/shard_map/dot_general | solution.py:8
  68.3 44.6 %all-gather.10.cloned.1.call-done = f32[1024,512]{1,0:T(8,128)} async-done(((f32[128,512]{1,0:T(8,128)}), f32[1024,512]{1,0:T(8,128)}) %all-gather.10.cloned.1.call-update) | async-done | bytes 2097168 | tf_op jit(solution)/shard_map/all_gather | solution.py:24
  112.9 5.7 %fusion.16 = f32[512,128]{1,0:T(8,128)} fusion(f32[1024,512]{1,0:T(8,128)} %all-gather.10.cloned.1.call-done, f32[1024,128]{1,0:T(8,128)S(1)} %copy-done), kind=kOutput, calls=%fused_computation.24 | convolution fusion | flops 805306368 | bytes 2883584 | tf_op jit(solution)/shard_map/dot_general | solution.py:8
  120.0 33.8 %all-gather.14.cloned.1.call-done = f32[1,512,512]{2,1,0:T(8,128)} async-done(((f32[1,64,512]{2,1,0:T(8,128)}), f32[1,512,512]{2,1,0:T(8,128)}) %all-gather.14.cloned.1.call-update) | async-done | bytes 1048592 | tf_op jit(solution)/shard_map/all_gather | solution.py:28
  153.9 35.1 %all-reduce.3.cloned.1.call-done = (f32[512,128]{1,0:T(8,128)}, f32[512,128]{1,0:T(8,128)}) async-done(((f32[512,128]{1,0:T(8,128)}, f32[512,128]{1,0:T(8,128)}), (f32[512,128]{1,0:T(8,128)}, f32[512,128]{1,0:T(8,128)})) %all-reduce.3.cloned.1.call-update) | async-done | bytes 524304 | tf_op jit(solution)/shard_map/psum | solution.py:25
  188.9 2.1 fusion.6
  191.0 1.0 fusion
  192.1 1.0 fusion.1
  193.1 38.2 %all-gather.12.cloned.1.call-done = f32[512,512]{1,0:T(8,128)} async-done(((f32[64,512]{1,0:T(8,128)}), f32[512,512]{1,0:T(8,128)}) %all-gather.12.cloned.1.call-update) | async-done | bytes 1048592 | tf_op jit(solution)/shard_map/all_gather | solution.py:44
  231.3 3.9 fusion.3
  235.2 37.7 %all-gather.16.cloned.1.call-done = f32[1,512,512]{2,1,0:T(8,128)} async-done(((f32[1,64,512]{2,1,0:T(8,128)}), f32[1,512,512]{2,1,0:T(8,128)}) %all-gather.16.cloned.1.call-update) | async-done | bytes 1048592 | tf_op jit(solution)/shard_map/all_gather | solution.py:28
  272.9 2.1 fusion.4
  275.7 1.0 fusion.2
  276.7 2.0 pad_maximum_fusion
  278.8 5.0 %convolution_negate_fusion = f32[1024,1024]{1,0:T(8,128)} fusion(f32[1024,128]{1,0:T(8,128)S(1)} %copy-done, f32[1024,128]{1,0:T(8,128)S(1)} %copy-done.1), kind=kOutput, calls=%fused_computation.1 | convolution fusion | flops 1611661312 | bytes 5242880 | tf_op jit(solution)/shard_map/dot_general | solution.py:31
  283.8 0.9 copy-done.3
  284.8 1.0 copy.10
  285.8 66.7 %reduce-scatter.5.cloned.1.call-done = f32[3,64,512]{2,1,0:T(8,128)} async-done(((f32[3,512,512]{2,1,0:T(8,128)}), f32[3,64,512]{2,1,0:T(8,128)}) %reduce-scatter.5.cloned.1.call-update) | async-done | bytes 393232 | tf_op jit(solution)/shard_map/reduce_scatter | solution.py:59
  352.5 1.7 slice.40
  354.1 1.6 slice_bitcast_fusion
  355.7 88.4 %reduce-scatter.3.cloned.1.call-done = f32[128,1024]{1,0:T(8,128)} async-done(((f32[1024,1024]{1,0:T(8,128)}), f32[128,1024]{1,0:T(8,128)}) %reduce-scatter.3.cloned.1.call-update) | async-done | bytes 524304 | tf_op jit(solution)/shard_map/reduce_scatter | solution.py:30
  (26 shorter events, 3.1 us)
Async XLA Ops:
  7.2 55.4 %copy-start = (f32[1024,128]{1,0:T(8,128)S(1)}, f32[1024,128]{1,0:T(8,128)}, u32[]{:S(2)}) copy-start(f32[1024,128]{1,0:T(8,128)} %param.8) | copy-start | bytes 1572868
  7.2 55.3 %all-gather.8.cloned.1.call-start = ((), (), s32[]{:S(2)}) async-start(), calls=%async_computation.2 | async-start | bytes 2359296 | tf_op jit(solution)/shard_map/all_gather | solution.py:24
  9.2 103.7 %all-gather.10.cloned.1.call-start = ((), (), s32[]{:S(2)}) async-start(), calls=%async_computation.3 | async-start | bytes 2359296 | tf_op jit(solution)/shard_map/all_gather | solution.py:24
  9.9 143.9 %all-gather.14.cloned.1.call-start = ((), (), s32[]{:S(2)}) async-start(), calls=%async_computation.7 | async-start | bytes 1179648 | tf_op jit(solution)/shard_map/all_gather | solution.py:28
  11.7 177.3 %copy-start.4 = (f32[1024,128]{1,0:T(8,128)S(1)}, f32[1024,128]{1,0:T(8,128)}, u32[]{:S(2)}) copy-start(f32[1024,128]{1,0:T(8,128)} %param.7) | copy-start | bytes 1572868
  11.7 177.3 %all-reduce.3.cloned.1.call-start = ((), (), s32[]{:S(2)}) async-start(), calls=%async_computation.9 | async-start | bytes 1048576 | tf_op jit(solution)/shard_map/psum | solution.py:25
  68.2 122.8 %copy-start.1 = (f32[1024,128]{1,0:T(8,128)S(1)}, f32[1024,128]{1,0:T(8,128)}, u32[]{:S(2)}) copy-start(f32[1024,128]{1,0:T(8,128)} %param.6) | copy-start | bytes 1572868
  118.6 112.7 %all-gather.12.cloned.1.call-start = ((), (), s32[]{:S(2)}) async-start(), calls=%async_computation.4 | async-start | bytes 1179648 | tf_op jit(solution)/shard_map/all_gather | solution.py:44
  119.2 153.7 %all-gather.16.cloned.1.call-start = ((), (), s32[]{:S(2)}) async-start(), calls=%async_computation.8 | async-start | bytes 1179648 | tf_op jit(solution)/shard_map/all_gather | solution.py:28
  119.8 232.7 %reduce-scatter.5.cloned.1.call-start = ((), (), s32[]{:S(2)}) async-start(), calls=%async_computation.6 | async-start | bytes 3538944 | tf_op jit(solution)/shard_map/reduce_scatter | solution.py:59
  275.0 0.7 copy-start.2
  278.7 165.3 %reduce-scatter.3.cloned.1.call-start = ((), (), s32[]{:S(2)}) async-start(), calls=%async_computation.5 | async-start | bytes 4718592 | tf_op jit(solution)/shard_map/reduce_scatter | solution.py:30
  283.8 1.0 copy-start.3
Sparse Core Ops, SparseCore 0:
  10.7 51.7 all-gather.7
  65.2 47.6 all-gather.9
  115.0 38.7 all-gather.13
  156.7 32.1 all-reduce.2
  190.9 40.3 all-gather.11
  233.9 38.9 all-gather.15
  278.9 73.5 reduce-scatter.4
  356.7 87.3 reduce-scatter.2
where the time goes:
time: 451 us
  waiting for transfers between devices  397 us (88%)
  matrix products  27.5 us (6%)
  between operations  14.2 us (3%)
  local copies, waits for them, and re-layouts  9.47 us (2%)
    all_gather x2, waiting for transfers between devices, below_correction(): lax.all_gather(columns, 'pair', axis=0, tiled=True)  95.4 us
    reduce_scatter x1, waiting for transfers between devices, body(): lax.psum_scatter(-lax.dot_general(bbar_below, x_panels, contract_cols, pr...  88.4 us
    all_gather x2, waiting for transfers between devices, solve_panel(): lax.all_gather(dinv[index], 'pair', axis=0, tiled=True)  71.6 us
    reduce_scatter x1, waiting for transfers between devices, body(): summed = lax.psum_scatter(stacked, 'pair', scatter_dimension=1, tiled=True)  66.7 us
    all_gather x1, waiting for transfers between devices, body(): lax.all_gather(l_cross, 'pair', axis=0, tiled=True)  38.2 us
    psum x1, waiting for transfers between devices, below_correction(): return lax.psum(folded, 'aux')  35.1 us
    dot_general x5, matrix products, fold_with(): lax.dot_general(pieces, right_side, (((0,), (0,)), ((), ())), precision=l...  19.4 us
  transfers between devices with their start and end apart: 8, of which 8 were waited for; matrix products, arithmetic and copies ran while one was open for 7% of the time, Pallas kernels for 0%

commit v1 on v0

--- a/solution.py
+++ b/solution.py
@@ -2,6 +2,23 @@
 import jax.numpy as jnp
 from jax import lax
 from jax.sharding import PartitionSpec as P
+
+
+def laid_out(blocks, dim):
+    shape = list(blocks.shape[1:])
+    shape[dim] *= blocks.shape[0]
+    return jnp.moveaxis(blocks, 0, dim).reshape(shape)
+
+
+def collect(x, axis, dim):
+    peers = lax.axis_size(axis)
+    right = [(i, (i + 1) % peers) for i in range(peers)]
+    pieces = [x]
+    while len(pieces) < peers:
+        pieces.append(lax.ppermute(pieces[-1], axis, right))
+    index = lax.axis_index(axis)
+    pieces = jnp.stack(pieces)[(index - jnp.arange(peers)) % peers]
+    return laid_out(pieces, dim)
 
 
 def fold_with(right_side, pieces):
@@ -41,7 +58,7 @@
     )
     late_corr = below_correction(panel, panel)
     bbar_late = solve_panel(1, xbar_panels[panel:] - late_corr)
-    cross_term = fold_with(bbar_late, lax.all_gather(l_cross, "pair", axis=0, tiled=True))
+    cross_term = fold_with(bbar_late, collect(l_cross, "pair", 0))
     early_corr = below_correction(0, panel)
     bbar_early = solve_panel(0, xbar_panels[:panel] - early_corr - cross_term)
     x_early = x_panels[:panel]

time: 451 us -> 415 us (0.920)
  waiting for transfers between devices: 397 us -> 360 us
    ppermute x0 -> x7, waiting for transfers between devices: none -> 56.3 us  [collect(): pieces.append(lax.ppermute(pieces[-1], axis, right))]
    all_gather x1 -> x0, waiting for transfers between devices: 38.2 us -> none  [body(): lax.all_gather(l_cross, 'pair', axis=0, tiled=True)]
    all_gather x2, waiting for transfers between devices: 71.6 us -> 35.2 us  [solve_panel(): lax.all_gather(dinv[index], 'pair', axis=0, tiled=True)]
    psum x1, waiting for transfers between devices: 35.1 us -> 16.9 us  [below_correction(): return lax.psum(folded, 'aux')]
  transfers between devices with their start and end apart: 8 -> 14, of which waited for: 8 -> 13; matrix products, arithmetic and copies ran while one was open for 7% -> 7% of each run, Pallas kernels for 0% -> 0%
where the time goes in v1:
time: 415 us; the launch traced here: 414 us
  waiting for transfers between devices  360 us (87%)
  matrix products  27.3 us (7%)
  between operations  14.3 us (3%)
  local copies, waits for them, and re-layouts  10.2 us (2%)
    all_gather x2, waiting for transfers between devices, below_correction(): lax.all_gather(columns, 'pair', axis=0, tiled=True)  95.4 us
    reduce_scatter x1, waiting for transfers between devices, body(): lax.psum_scatter(-lax.dot_general(bbar_below, x_panels, contract_cols, pr...  88.4 us
    reduce_scatter x1, waiting for transfers between devices, body(): summed = lax.psum_scatter(stacked, 'pair', scatter_dimension=1, tiled=True)  66.7 us
    ppermute x7, waiting for transfers between devices, collect(): pieces.append(lax.ppermute(pieces[-1], axis, right))  56.3 us
    all_gather x2, waiting for transfers between devices, solve_panel(): lax.all_gather(dinv[index], 'pair', axis=0, tiled=True)  35.2 us
    dot_general x5, matrix products, fold_with(): lax.dot_general(pieces, right_side, (((0,), (0,)), ((), ())), precision=l...  18.2 us
    psum x1, waiting for transfers between devices, below_correction(): return lax.psum(folded, 'aux')  16.9 us
  transfers between devices with their start and end apart: 14, of which 13 were waited for; matrix products, arithmetic and copies ran while one was open for 7% of the time, Pallas kernels for 0%

profile of v1, /device:TPU:0, one launch (start us, length us, event | category | flops | bytes accessed | tf_op | source)
XLA Modules:
  0.0 414.5 jit_solution(10675080695404824150)
XLA Ops:
  7.2 1.9 fusion.14
  10.0 1.7 fusion.15
  11.7 50.8 %all-gather.7.cloned.1.call-done = f32[1024,512]{1,0:T(8,128)} async-done(((f32[128,512]{1,0:T(8,128)}), f32[1024,512]{1,0:T(8,128)}) %all-gather.7.cloned.1.call-update) | async-done | bytes 2097168 | tf_op jit(solution)/shard_map/all_gather | solution.py:41
  62.5 5.7 %fusion.16 = f32[512,128]{1,0:T(8,128)} fusion(f32[1024,512]{1,0:T(8,128)} %all-gather.7.cloned.1.call-done, f32[1024,128]{1,0:T(8,128)S(1)} %copy-done), kind=kOutput, calls=%fused_computation.38 | convolution fusion | flops 805306368 | bytes 2883584 | tf_op jit(solution)/shard_map/dot_general | solution.py:25
  68.2 44.6 %all-gather.9.cloned.1.call-done = f32[1024,512]{1,0:T(8,128)} async-done(((f32[128,512]{1,0:T(8,128)}), f32[1024,512]{1,0:T(8,128)}) %all-gather.9.cloned.1.call-update) | async-done | bytes 2097168 | tf_op jit(solution)/shard_map/all_gather | solution.py:41
  112.9 5.7 %fusion.17 = f32[512,128]{1,0:T(8,128)} fusion(f32[1024,512]{1,0:T(8,128)} %all-gather.9.cloned.1.call-done, f32[1024,128]{1,0:T(8,128)S(1)} %copy-done), kind=kOutput, calls=%fused_computation.39 | convolution fusion | flops 805306368 | bytes 2883584 | tf_op jit(solution)/shard_map/dot_general | solution.py:25
  119.4 7.1 %collective-permute-done = f32[64,512]{1,0:T(8,128)S(1)} collective-permute-done((f32[64,512]{1,0:T(8,128)S(1)}, f32[64,512]{1,0:T(8,128)S(1)}, u32[]{:S(2)}, u32[]{:S(2)}) %collective-permute-start) | collective-permute-done | bytes 131104 | tf_op jit(solution)/shard_map/ppermute | solution.py:18
  126.6 7.9 %collective-permute-done.1 = f32[64,512]{1,0:T(8,128)S(1)} collective-permute-done((f32[64,512]{1,0:T(8,128)S(1)}, f32[64,512]{1,0:T(8,128)S(1)}, u32[]{:S(2)}, u32[]{:S(2)}) %collective-permute-start.1) | collective-permute-done | bytes 131104 | tf_op jit(solution)/shard_map/ppermute | solution.py:18
  134.5 7.9 %collective-permute-done.2 = f32[64,512]{1,0:T(8,128)S(1)} collective-permute-done((f32[64,512]{1,0:T(8,128)S(1)}, f32[64,512]{1,0:T(8,128)S(1)}, u32[]{:S(2)}, u32[]{:S(2)}) %collective-permute-start.2) | collective-permute-done | bytes 131104 | tf_op jit(solution)/shard_map/ppermute | solution.py:18
  142.4 9.9 %collective-permute-done.3 = f32[64,512]{1,0:T(8,128)S(1)} collective-permute-done((f32[64,512]{1,0:T(8,128)S(1)}, f32[64,512]{1,0:T(8,128)S(1)}, u32[]{:S(2)}, u32[]{:S(2)}) %collective-permute-start.3) | collective-permute-done | bytes 131104 | tf_op jit(solution)/shard_map/ppermute | solution.py:18
  152.3 8.2 %collective-permute-done.4 = f32[64,512]{1,0:T(8,128)S(1)} collective-permute-done((f32[64,512]{1,0:T(8,128)S(1)}, f32[64,512]{1,0:T(8,128)S(1)}, u32[]{:S(2)}, u32[]{:S(2)}) %collective-permute-start.4) | collective-permute-done | bytes 131104 | tf_op jit(solution)/shard_map/ppermute | solution.py:18
  160.5 7.6 %collective-permute-done.5 = f32[64,512]{1,0:T(8,128)S(1)} collective-permute-done((f32[64,512]{1,0:T(8,128)S(1)}, f32[64,512]{1,0:T(8,128)S(1)}, u32[]{:S(2)}, u32[]{:S(2)}) %collective-permute-start.5) | collective-permute-done | bytes 131104 | tf_op jit(solution)/shard_map/ppermute | solution.py:18
  168.2 7.6 %collective-permute-done.6 = f32[64,512]{1,0:T(8,128)S(1)} collective-permute-done((f32[64,512]{1,0:T(8,128)S(1)}, f32[64,512]{1,0:T(8,128)S(1)}, u32[]{:S(2)}, u32[]{:S(2)}) %collective-permute-start.6) | collective-permute-done | bytes 131104 | tf_op jit(solution)/shard_map/ppermute | solution.py:18
  176.5 16.9 %all-reduce.3.cloned.1.call-done = (f32[512,128]{1,0:T(8,128)}, f32[512,128]{1,0:T(8,128)}) async-done(((f32[512,128]{1,0:T(8,128)}, f32[512,128]{1,0:T(8,128)}), (f32[512,128]{1,0:T(8,128)}, f32[512,128]{1,0:T(8,128)})) %all-reduce.3.cloned.1.call-update) | async-done | bytes 524304 | tf_op jit(solution)/shard_map/psum | solution.py:42
  193.4 2.2 fusion.5
  196.7 2.0 fusion.1
  198.7 2.5 convolution_subtract_fusion
  201.2 35.2 %all-gather.13.cloned.1.call-done = f32[1,512,512]{2,1,0:T(8,128)} async-done(((f32[1,64,512]{2,1,0:T(8,128)}), f32[1,512,512]{2,1,0:T(8,128)}) %all-gather.13.cloned.1.call-update) | async-done | bytes 1048592 | tf_op jit(solution)/shard_map/all_gather | solution.py:45
  236.4 2.1 fusion.3
  240.2 2.0 pad_maximum_fusion
  242.2 5.0 %convolution_negate_fusion = f32[1024,1024]{1,0:T(8,128)} fusion(f32[1024,128]{1,0:T(8,128)S(1)} %copy-done, f32[1024,128]{1,0:T(8,128)S(1)} %copy-done.2), kind=kOutput, calls=%fused_computation.2 | convolution fusion | flops 1611661312 | bytes 5242880 | tf_op jit(solution)/shard_map/dot_general | solution.py:48
  249.3 66.7 %reduce-scatter.5.cloned.1.call-done = f32[3,64,512]{2,1,0:T(8,128)} async-done(((f32[3,512,512]{2,1,0:T(8,128)}), f32[3,64,512]{2,1,0:T(8,128)}) %reduce-scatter.5.cloned.1.call-update) | async-done | bytes 393232 | tf_op jit(solution)/shard_map/reduce_scatter | solution.py:76
  316.0 1.7 slice.42
  319.2 88.4 %reduce-scatter.3.cloned.1.call-done = f32[128,1024]{1,0:T(8,128)} async-done(((f32[1024,1024]{1,0:T(8,128)}), f32[128,1024]{1,0:T(8,128)}) %reduce-scatter.3.cloned.1.call-update) | async-done | bytes 524304 | tf_op jit(solution)/shard_map/reduce_scatter | solution.py:47
  (54 shorter events, 8.8 us)
Async XLA Ops:
  7.2 55.4 %copy-start = (f32[1024,128]{1,0:T(8,128)S(1)}, f32[1024,128]{1,0:T(8,128)}, u32[]{:S(2)}) copy-start(f32[1024,128]{1,0:T(8,128)} %param.8) | copy-start | bytes 1572868
  7.2 55.3 %all-gather.7.cloned.1.call-start = ((), (), s32[]{:S(2)}) async-start(), calls=%async_computation.2 | async-start | bytes 2359296 | tf_op jit(solution)/shard_map/all_gather | solution.py:41
  9.2 103.7 %all-gather.9.cloned.1.call-start = ((), (), s32[]{:S(2)}) async-start(), calls=%async_computation.3 | async-start | bytes 2359296 | tf_op jit(solution)/shard_map/all_gather | solution.py:41
  9.9 166.6 %all-gather.11.cloned.1.call-start = ((), (), s32[]{:S(2)}) async-start(), calls=%async_computation.6 | async-start | bytes 1179648 | tf_op jit(solution)/shard_map/all_gather | solution.py:45
  11.7 107.0 %copy-start.7 = (f32[64,512]{1,0:T(8,128)S(1)}, f32[64,512]{1,0:T(8,128)}, u32[]{:S(2)}) copy-start(f32[64,512]{1,0:T(8,128)} %param.10) | copy-start | bytes 393220
  11.7 181.7 %all-reduce.3.cloned.1.call-start = ((), (), s32[]{:S(2)}) async-start(), calls=%async_computation.8 | async-start | bytes 1048576 | tf_op jit(solution)/shard_map/psum | solution.py:42
  118.6 77.0 %copy-start.2 = (f32[1024,128]{1,0:T(8,128)S(1)}, f32[1024,128]{1,0:T(8,128)}, u32[]{:S(2)}) copy-start(f32[1024,128]{1,0:T(8,128)} %param.6) | copy-start | bytes 1572868
  118.6 117.7 %all-gather.13.cloned.1.call-start = ((), (), s32[]{:S(2)}) async-start(), calls=%async_computation.7 | async-start | bytes 1179648 | tf_op jit(solution)/shard_map/all_gather | solution.py:45
  118.7 7.8 %collective-permute-start = (f32[64,512]{1,0:T(8,128)S(1)}, f32[64,512]{1,0:T(8,128)S(1)}, u32[]{:S(2)}, u32[]{:S(2)}) collective-permute-start(f32[64,512]{1,0:T(8,128)S(1)} %copy-done.7), channel_id=1, source_target_pairs={{0,4},{4,8},{8,12},{12,16},{16,20},{20,24},{24,28},{28,0},{1,5},{5... | collective-permute-start | bytes 393224 | tf_op jit(solution)/shard_map/ppermute | solution.py:18
  119.3 196.6 %reduce-scatter.5.cloned.1.call-start = ((), (), s32[]{:S(2)}) async-start(), calls=%async_computation.5 | async-start | bytes 3538944 | tf_op jit(solution)/shard_map/reduce_scatter | solution.py:76
  126.5 7.9 %collective-permute-start.1 = (f32[64,512]{1,0:T(8,128)S(1)}, f32[64,512]{1,0:T(8,128)S(1)}, u32[]{:S(2)}, u32[]{:S(2)}) collective-permute-start(f32[64,512]{1,0:T(8,128)S(1)} %collective-permute-done), channel_id=1, source_target_pairs={{0,4},{4,8},{8,12},{12,16},{16,20},{20,24},{24,28},{28,0},{1,5},{5... | collective-permute-start | bytes 393224 | tf_op jit(solution)/shard_map/ppermute | solution.py:18
  134.4 7.9 %collective-permute-start.2 = (f32[64,512]{1,0:T(8,128)S(1)}, f32[64,512]{1,0:T(8,128)S(1)}, u32[]{:S(2)}, u32[]{:S(2)}) collective-permute-start(f32[64,512]{1,0:T(8,128)S(1)} %collective-permute-done.1), channel_id=1, source_target_pairs={{0,4},{4,8},{8,12},{12,16},{16,20},{20,24},{24,28},{28,0},{1,5},{5... | collective-permute-start | bytes 393224 | tf_op jit(solution)/shard_map/ppermute | solution.py:18
  142.4 9.9 %collective-permute-start.3 = (f32[64,512]{1,0:T(8,128)S(1)}, f32[64,512]{1,0:T(8,128)S(1)}, u32[]{:S(2)}, u32[]{:S(2)}) collective-permute-start(f32[64,512]{1,0:T(8,128)S(1)} %collective-permute-done.2), channel_id=1, source_target_pairs={{0,4},{4,8},{8,12},{12,16},{16,20},{20,24},{24,28},{28,0},{1,5},{5... | collective-permute-start | bytes 393224 | tf_op jit(solution)/shard_map/ppermute | solution.py:18
  152.3 8.2 %collective-permute-start.4 = (f32[64,512]{1,0:T(8,128)S(1)}, f32[64,512]{1,0:T(8,128)S(1)}, u32[]{:S(2)}, u32[]{:S(2)}) collective-permute-start(f32[64,512]{1,0:T(8,128)S(1)} %collective-permute-done.3), channel_id=1, source_target_pairs={{0,4},{4,8},{8,12},{12,16},{16,20},{20,24},{24,28},{28,0},{1,5},{5... | collective-permute-start | bytes 393224 | tf_op jit(solution)/shard_map/ppermute | solution.py:18
  160.5 7.7 %collective-permute-start.5 = (f32[64,512]{1,0:T(8,128)S(1)}, f32[64,512]{1,0:T(8,128)S(1)}, u32[]{:S(2)}, u32[]{:S(2)}) collective-permute-start(f32[64,512]{1,0:T(8,128)S(1)} %collective-permute-done.4), channel_id=1, source_target_pairs={{0,4},{4,8},{8,12},{12,16},{16,20},{20,24},{24,28},{28,0},{1,5},{5... | collective-permute-start | bytes 393224 | tf_op jit(solution)/shard_map/ppermute | solution.py:18
  168.2 7.7 %collective-permute-start.6 = (f32[64,512]{1,0:T(8,128)S(1)}, f32[64,512]{1,0:T(8,128)S(1)}, u32[]{:S(2)}, u32[]{:S(2)}) collective-permute-start(f32[64,512]{1,0:T(8,128)S(1)} %collective-permute-done.5), channel_id=1, source_target_pairs={{0,4},{4,8},{8,12},{12,16},{16,20},{20,24},{24,28},{28,0},{1,5},{5... | collective-permute-start | bytes 393224 | tf_op jit(solution)/shard_map/ppermute | solution.py:18
  193.4 5.3 %copy-start.5 = (f32[1024,128]{1,0:T(8,128)S(1)}, f32[1024,128]{1,0:T(8,128)}, u32[]{:S(2)}) copy-start(f32[1024,128]{1,0:T(8,128)} %param.7) | copy-start | bytes 1572868
  193.4 5.3 %copy-start.6 = (f32[512,128]{1,0:T(8,128)S(1)}, f32[512,128]{1,0:T(8,128)}, u32[]{:S(2)}) copy-start(f32[512,128]{1,0:T(8,128)} %get-tuple-element.9) | copy-start | bytes 786436
  201.2 39.0 %copy-start.1 = (f32[1,512,512]{2,1,0:T(8,128)S(1)}, f32[1,512,512]{2,1,0:T(8,128)}, u32[]{:S(2)}) copy-start(f32[1,512,512]{2,1,0:T(8,128)} %fusion.1) | copy-start | bytes 3145732
  238.5 0.7 copy-start.3
  242.2 165.4 %reduce-scatter.3.cloned.1.call-start = ((), (), s32[]{:S(2)}) async-start(), calls=%async_computation.4 | async-start | bytes 4718592 | tf_op jit(solution)/shard_map/reduce_scatter | solution.py:47
  247.3 1.0 copy-start.4
Sparse Core Ops, SparseCore 0:
  10.7 51.7 all-gather.6
  65.2 47.6 all-gather.8
  115.0 41.4 all-gather.10
  159.4 33.9 all-reduce.2
  195.9 40.3 all-gather.12
  242.3 73.5 reduce-scatter.4
  320.2 87.4 reduce-scatter.2
